TPU v7x, 32 devices: a whole 2x2x4 slice. The times are simulated.
32 devices in a mesh: ctx: 4 (over y, x), exp: 8 (over z, core).
Axes of the slice: x: 2, y: 2, z: 4, core: 2. Of those that a mesh axis runs over, the one named last changes fastest.
Arguments:
- hidden_in: bfloat16 [1024, 2048], P(('ctx', 'exp')), may hold values from -6 to 6
- queries: bfloat16 [1024, 4096], P('ctx', 'exp'), may hold values from -200 to 200
- keyvals: bfloat16 [1024, 512], P('ctx'), may hold values from -6 to 6
- out_weight: bfloat16 [4096, 2048], P('exp'), may hold values from -0.09375 to 0.09375
- norm_gain: float32 [2048], replicated, may hold values from 0.5 to 1.5
- router_weight: bfloat16 [2048, 16], replicated, may hold values from -0.125 to 0.125
- expert_gate_up: bfloat16 [16, 2048, 1536], P('exp', 'ctx'), may hold values from -0.125 to 0.125
- expert_down: bfloat16 [16, 768, 2048], P('exp', 'ctx'), may hold values from -0.21875 to 0.21875
- route_ids: int32 [1024, 8], P(('ctx', 'exp')), may hold values from 0 to 15, all different within a row; in each aligned block of 32 rows (0 to 31, 32 to 63, ...) at most 18 rows name the same one
- upstream: bfloat16 [1024, 2048], P(('ctx', 'exp')), may hold values from -6 to 6
Outputs:
- layer_out: bfloat16 [1024, 2048], P(('ctx', 'exp'))
- input_grad: bfloat16 [1024, 2048], P(('ctx', 'exp'))
- query_grad: bfloat16 [1024, 4096], P('ctx', 'exp')
- out_weight_grad: float32 [4096, 2048], P('exp', 'ctx')
- gate_up_grad: float32 [16, 2048, 1536], P('exp', 'ctx')
- down_grad: float32 [16, 768, 2048], P('exp', 'ctx')
- router_grad: float32 [2048, 16], replicated
- gain_grad: float32 [2048], replicated
Inputs may be any that keep to these rules, and one draw needn't show every extreme that they name: `route_ids`: each row names 8 different experts. In each aligned block of 32 rows (the rows of one device) no expert is named by more than 18 rows, a bound that some block reaches.
All inputs are finite; a program needn't handle non-finite values.
Results may differ from a plain program's by a relative error of at most 0.02.
Values may be sent and summed in bfloat16 or wider, within the bound.
A program may use at most 128 MiB of HBM per device.

v0:
```python
import jax
import jax.numpy as jnp
from jax import lax
from jax.sharding import PartitionSpec as P

HEAD_WIDTH = 128
QUERY_HEADS = 32
KEY_VALUE_HEADS = 2
FFE = 768
EXPERTS = 16
norm_eps = 1e-06


def per_device(
    hidden_in,
    queries,
    keyvals,
    out_weight,
    norm_gain,
    router_weight,
    expert_gate_up,
    expert_down,
    route_ids,
    upstream,
):
    exp_count = lax.axis_size("exp")
    ctx_index = lax.axis_index("ctx")
    exp_index = lax.axis_index("exp")
    tok_ctx = queries.shape[0]
    tok_dev = hidden_in.shape[0]
    local_heads = queries.shape[1] // HEAD_WIDTH
    local_experts = EXPERTS // exp_count
    score_scale = HEAD_WIDTH ** (-0.5)
    keyvalue_head = exp_index * local_heads // (QUERY_HEADS // KEY_VALUE_HEADS)
    own_block = lax.dynamic_slice_in_dim(keyvals, keyvalue_head * 2 * HEAD_WIDTH, 2 * HEAD_WIDTH, 1)
    all_kv = lax.all_gather(own_block, "ctx", axis=0, tiled=True)
    ids_block = lax.all_gather(route_ids, "exp", axis=0, tiled=True)
    upstream_block = lax.all_gather(upstream, "exp", axis=0, tiled=True)
    gate_up_full = lax.all_gather(expert_gate_up, "ctx", axis=1, tiled=True)
    down_full = lax.all_gather(expert_down, "ctx", axis=1, tiled=True)
    upstream_all = lax.all_gather(upstream_block, "ctx", axis=0, tiled=True)
    keys, values = (all_kv[:, :HEAD_WIDTH], all_kv[:, HEAD_WIDTH:])
    query_pos = ctx_index * tok_ctx + jnp.arange(tok_ctx, dtype=jnp.int32)
    key_pos = jnp.arange(keys.shape[0], dtype=jnp.int32)
    allowed = key_pos[None, :] <= query_pos[:, None]

    def columns(array, head):
        return array[:, head * HEAD_WIDTH : (head + 1) * HEAD_WIDTH]

    def dot_t(a, b):
        return lax.dot_general(a, b, (((1,), (1,)), ((), ())), preferred_element_type=jnp.float32)

    def head_scores(head):
        return jnp.where(allowed, dot_t(columns(queries, head), keys) * score_scale, -jnp.inf)

    attention_heads, log_totals = ([], [])
    for head in range(local_heads):
        scores = head_scores(head)
        row_max = jnp.max(scores, axis=1, keepdims=True)
        weights = jnp.exp(scores - row_max)
        row_sum = jnp.sum(weights, axis=1, keepdims=True)
        mixed = jnp.dot(weights.astype(jnp.bfloat16), values, preferred_element_type=jnp.float32)
        attention_heads.append((mixed / row_sum).astype(jnp.bfloat16))
        log_totals.append(row_max + jnp.log(row_sum))
    attention_flat = jnp.concatenate(attention_heads, axis=1)
    attention_all = lax.all_gather(attention_flat, "ctx", axis=0, tiled=True)
    projected = lax.psum_scatter(
        jnp.dot(attention_flat, out_weight, preferred_element_type=jnp.float32).astype(
            jnp.bfloat16
        ),
        "exp",
        scatter_dimension=0,
        tiled=True,
    ).astype(jnp.float32)
    residual = hidden_in.astype(jnp.float32) + projected
    inv_rms = lax.rsqrt(jnp.mean(residual * residual, axis=1, keepdims=True) + norm_eps)
    normed = (residual * inv_rms * norm_gain).astype(jnp.bfloat16)
    normed_block = lax.all_gather(normed, "exp", axis=0, tiled=True)
    normed_cols = lax.all_to_all(normed_block, "ctx", split_axis=1, concat_axis=0, tiled=True)
    logits = jnp.dot(normed_block, router_weight, preferred_element_type=jnp.float32)
    expert_ids = jnp.arange(EXPERTS, dtype=jnp.int32)
    hit_block = jnp.any(ids_block[:, :, None] == expert_ids, axis=1)
    masked = jnp.where(hit_block, logits, -jnp.inf)
    shifted = jnp.exp(masked - jnp.max(masked, axis=1, keepdims=True))
    probs_block = shifted / jnp.sum(shifted, axis=1, keepdims=True)
    probs_here = lax.dynamic_slice_in_dim(probs_block, exp_index * local_experts, local_experts, 1)
    probs_cols = probs_here.T[:, :, None]
    out_grad_block = upstream_block.astype(jnp.float32)
    row_grads = (probs_cols * out_grad_block[None]).astype(jnp.bfloat16)
    gate_up = jnp.einsum(
        "td,edf->etf", normed_block, gate_up_full, preferred_element_type=jnp.float32
    )
    gate_part = gate_up[:, :, :FFE]
    up_part = gate_up[:, :, FFE:]
    sigmoid_gate = jax.nn.sigmoid(gate_part)
    activation = (gate_part * sigmoid_gate * up_part).astype(jnp.bfloat16)
    scaled_act = (probs_cols * activation.astype(jnp.float32)).astype(jnp.bfloat16)
    act_grad = jnp.einsum("etd,efd->etf", row_grads, down_full, preferred_element_type=jnp.float32)
    gate_grad = act_grad * up_part * sigmoid_gate * (1.0 + gate_part * (1.0 - sigmoid_gate))
    up_grad = act_grad * gate_part * sigmoid_gate
    pair_grad = jnp.concatenate([gate_grad, up_grad], axis=2).astype(jnp.bfloat16)
    pair_grad_all = lax.all_gather(pair_grad, "ctx", axis=1, tiled=True)
    rows_back = jnp.einsum(
        "etf,edf->td", pair_grad, gate_up_full, preferred_element_type=jnp.float32
    )
    expert_part = lax.psum_scatter(
        rows_back.astype(jnp.bfloat16), "exp", scatter_dimension=0, tiled=True
    ).astype(jnp.float32)
    expert_out = (
        jnp.einsum("etf,efd->etd", activation, down_full, preferred_element_type=jnp.float32)
        .astype(jnp.bfloat16)
        .astype(jnp.float32)
    )
    prob_grads_here = jnp.sum(expert_out * out_grad_block[None], axis=2)
    prob_grads = lax.all_to_all(prob_grads_here, "exp", split_axis=1, concat_axis=0, tiled=True).T
    mixture = lax.psum_scatter(
        jnp.sum(probs_cols * expert_out, axis=0).astype(jnp.bfloat16),
        "exp",
        scatter_dimension=0,
        tiled=True,
    ).astype(jnp.float32)
    layer_out = (residual + mixture).astype(jnp.bfloat16)
    act_rows = lax.all_to_all(
        jnp.swapaxes(scaled_act, 1, 2), "ctx", split_axis=1, concat_axis=2, tiled=True
    )
    down_grad = jnp.einsum(
        "eft,td->efd", act_rows, upstream_all, preferred_element_type=jnp.float32
    )
    gate_up_grad = jnp.einsum(
        "td,etf->edf", normed_cols, pair_grad_all, preferred_element_type=jnp.float32
    )
    out_grad = upstream.astype(jnp.float32)
    probs = lax.dynamic_slice_in_dim(probs_block, exp_index * tok_dev, tok_dev, 0)
    logit_grad = probs * (prob_grads - jnp.sum(probs * prob_grads, axis=1, keepdims=True))
    router_term = jnp.einsum(
        "te,td->ed", logit_grad, normed.astype(jnp.float32), precision=lax.Precision.HIGHEST
    )
    normed_grad = expert_part + jnp.einsum(
        "te,de->td", logit_grad, router_weight.astype(jnp.float32), precision=lax.Precision.HIGHEST
    )
    gain_term = jnp.sum(normed_grad * residual * inv_rms, axis=0, keepdims=True)
    summed = lax.psum(jnp.concatenate([router_term, gain_term], axis=0), ("ctx", "exp"))
    router_grad, gain_grad = (summed[:EXPERTS].T, summed[EXPERTS])
    inner_mean = jnp.mean(residual * norm_gain * normed_grad, axis=1, keepdims=True)
    input_grad = (
        out_grad + norm_gain * inv_rms * normed_grad - residual * inv_rms**3 * inner_mean
    ).astype(jnp.bfloat16)
    arriving = lax.all_gather(input_grad, "exp", axis=0, tiled=True)
    arriving_cols = lax.all_to_all(arriving, "ctx", split_axis=1, concat_axis=0, tiled=True)
    out_weight_grad = jnp.einsum(
        "tc,td->cd", attention_all, arriving_cols, preferred_element_type=jnp.float32
    )
    attention_grad = dot_t(arriving, out_weight).astype(jnp.bfloat16)
    query_grads = []
    for head in range(local_heads):
        grad_head = columns(attention_grad, head)
        delta = jnp.sum(
            grad_head.astype(jnp.float32) * attention_heads[head].astype(jnp.float32),
            axis=1,
            keepdims=True,
        )
        attn_probs = jnp.exp(head_scores(head) - log_totals[head])
        score_grad = (attn_probs * (dot_t(grad_head, values) - delta)).astype(jnp.bfloat16)
        query_acc = jnp.dot(score_grad, keys, preferred_element_type=jnp.float32)
        query_grads.append((score_scale * query_acc).astype(jnp.bfloat16))
    query_grad = jnp.concatenate(query_grads, axis=1)
    return (
        layer_out,
        input_grad,
        query_grad,
        out_weight_grad,
        gate_up_grad,
        down_grad,
        router_grad,
        gain_grad,
    )


def solution(mesh):
    return jax.shard_map(
        per_device,
        mesh=mesh,
        in_specs=(
            P(("ctx", "exp"), None),
            P("ctx", "exp"),
            P("ctx", None),
            P("exp", None),
            P(),
            P(),
            P("exp", "ctx", None),
            P("exp", "ctx", None),
            P(("ctx", "exp"), None),
            P(("ctx", "exp"), None),
        ),
        out_specs=(
            P(("ctx", "exp"), None),
            P(("ctx", "exp"), None),
            P("ctx", "exp"),
            P("exp", "ctx"),
            P("exp", "ctx", None),
            P("exp", "ctx", None),
            P(),
            P(),
        ),
        check_vma=False,
    )
```

profile of v0, /device:TPU:0, one launch (start us, length us, event | category | flops | bytes accessed | tf_op | source)
XLA Modules:
  0.0 746.0 jit_solution(9986827355923564355)
XLA Ops:
  8.3 11.5 %all_gather.30 = bf16[1024,256]{1,0:T(8,128)(2,1)S(1)} all-gather(bf16[256,256]{1,0:T(8,128)(2,1)S(1)} %constant_dynamic-slice_fusion), channel_id=1, replica_groups=mesh['ctx'=4,'exp'=8] {'ctx'}, dimensions={0}, use_global_device_ids=true | all-gather | bytes 655360 | tf_op jit(solution)/shard_map/all_gather | solution.py:36
  21.1 1.3 fusion.114
  25.8 1.7 convolution_convert_fusion.1
  28.3 32.2 %reduce-scatter.4.cloned.1.call-done = bf16[32,2048]{1,0:T(8,128)(2,1)} async-done(((bf16[256,2048]{1,0:T(8,128)(2,1)}), bf16[32,2048]{1,0:T(8,128)(2,1)}) %reduce-scatter.4.cloned.1.call-update) | async-done | bytes 131088 | tf_op jit(solution)/shard_map/reduce_scatter | solution.py:67
  62.2 1.6 multiply_convert_fusion.6
  65.1 14.4 %all-gather = s32[8,32,8]{1,2,0:T(8,128)S(1)} all-gather(s32[1,32,8]{1,2,0:T(8,128)S(1)} %bitcast.93), channel_id=1, replica_groups=mesh['ctx'=4,'exp'=8] {'exp'}, dimensions={0}, use_global_device_ids=true | all-gather | bytes 9216 | tf_op jit(solution)/shard_map/all_gather | solution.py:37
  79.6 2.9 all-gather.16.cloned.1.call-done
  82.5 2.8 convert_element_type.151
  85.3 21.3 %all-gather.10.cloned.1.call-done = bf16[256,2048]{1,0:T(8,128)(2,1)} async-done(((bf16[32,2048]{1,0:T(8,128)(2,1)}), bf16[256,2048]{1,0:T(8,128)(2,1)}) %all-gather.10.cloned.1.call-update) | async-done | bytes 1048592 | tf_op jit(solution)/shard_map/all_gather | solution.py:78
  106.6 1.6 fusion.116
  108.3 122.0 %all-gather.12.cloned.1.call-done = bf16[2,2048,1536]{2,1,0:T(8,128)(2,1)} async-done(((bf16[2,512,1536]{2,1,0:T(8,128)(2,1)}), bf16[2,2048,1536]{2,1,0:T(8,128)(2,1)}) %all-gather.12.cloned.1.call-update) | async-done | bytes 12582928 | tf_op jit(solution)/shard_map/all_gather | solution.py:39
  230.4 10.0 %convolution_bitcast_fusion.1 = f32[2,256,1536]{2,1,0:T(8,128)} fusion(bf16[2,2048,1536]{2,1,0:T(8,128)(2,1)} %all-gather.12.cloned.1.call-done, bf16[256,2048]{1,0:T(8,128)(2,1)} %all-gather.10.cloned.1.call-done), kind=kOutput, calls=%fused_computation.8 | convolution fusion | flops 3221225472 | bytes 16777216 | tf_op jit(solution)/shard_map/td,edf->etf/dot_general | solution.py:90
  240.3 61.8 %all-gather.14.cloned.1.call-done = bf16[2,768,2048]{2,1,0:T(8,128)(2,1)} async-done(((bf16[2,192,2048]{2,1,0:T(8,128)(2,1)}), bf16[2,768,2048]{2,1,0:T(8,128)(2,1)}) %all-gather.14.cloned.1.call-update) | async-done | bytes 6291472 | tf_op jit(solution)/shard_map/all_gather | solution.py:40
  302.1 9.5 %multiply_convert_fusion.4 = (bf16[2,256,768]{2,1,0:T(8,128)(2,1)S(1)}, bf16[2,256,768]{2,1,0:T(8,128)(2,1)S(1)}, bf16[2,768,256]{1,2,0:T(8,128)(2,1)}, bf16[2,256,768]{2,1,0:T(8,128)(2,1)}) fusion(f32[2,256,1536]{2,1,0:T(8,128)} %convolution_bitcast_fusion.1, f32[2,256]{1,0:T(2,128)S(1)} %dynamic-slice_bitcast_fusion, ...), kind=kOutput, calls=%fused_computation.20 | convolution fusion | flops 1620180992 | bytes 14684160 | tf_op jit(solution)/shard_map/etd,efd->etf/dot_general | solution.py:98
  312.4 9.0 %fusion.4 = bf16[256,2048]{1,0:T(8,128)(2,1)} fusion(bf16[2,2048,1536]{2,1,0:T(8,128)(2,1)} %all-gather.12.cloned.1.call-done, bf16[2,256,768]{2,1,0:T(8,128)(2,1)S(1)} %get-tuple-element.51, bf16[2,256,768]{2,1,0:T(8,128)(2,1)S(1)} %get-tuple-element.50), kind=kOutput, calls=%fused_computation.12 | convolution fusion | flops 3224895488 | bytes 15204352 | tf_op jit(solution)/shard_map/etf,edf->td/dot_general | solution.py:103
  321.5 7.0 fusion.1
  329.9 4.6 all-to-all-start
  334.6 5.6 all-to-all-done
  341.2 13.0 %reduce-scatter.8.cloned.1.call-done = bf16[32,2048]{1,0:T(8,128)(2,1)} async-done(((bf16[256,2048]{1,0:T(8,128)(2,1)}), bf16[32,2048]{1,0:T(8,128)(2,1)}) %reduce-scatter.8.cloned.1.call-update) | async-done | bytes 131088 | tf_op jit(solution)/shard_map/reduce_scatter | solution.py:106
  354.2 1.5 multiply_reduce_fusion
  356.2 1.6 pad_maximum_fusion.3
  357.9 30.1 %reduce-scatter.6.cloned.1.call-done = bf16[32,2048]{1,0:T(8,128)(2,1)} async-done(((bf16[256,2048]{1,0:T(8,128)(2,1)}), bf16[32,2048]{1,0:T(8,128)(2,1)}) %reduce-scatter.6.cloned.1.call-update) | async-done | bytes 131088 | tf_op jit(solution)/shard_map/reduce_scatter | solution.py:116
  388.0 1.8 subtract_convert_fusion
  389.9 1.6 pad_maximum_fusion.1
  391.6 2.4 pad_maximum_fusion
  394.6 3.1 copy.61
  397.7 4.4 all-to-all-start.3
  405.0 13.4 %all-to-all-done.3 = bf16[2,768,256]{2,0,1:T(2,128)(2,1)} async-done(((bf16[2,768,256]{2,0,1:T(2,128)(2,1)}), bf16[2,768,256]{2,0,1:T(2,128)(2,1)}, u32[]{:S(2)}, u32[]{:S(2)}) %all-to-all-start.3) | async-done | bytes 786464 | tf_op jit(solution)/shard_map/all_to_all | solution.py:123
  419.7 29.4 %all-gather.24.cloned.1.call-done = bf16[1024,2048]{1,0:T(8,128)(2,1)} async-done(((bf16[256,2048]{1,0:T(8,128)(2,1)}), bf16[1024,2048]{1,0:T(8,128)(2,1)}) %all-gather.24.cloned.1.call-update) | async-done | bytes 4194320 | tf_op jit(solution)/shard_map/all_gather | solution.py:41
  449.1 5.6 fusion.2
  454.8 125.2 %all-reduce.2.cloned.1.call-done = f32[17,2048]{1,0:T(8,128)} async-done(((f32[17,2048]{1,0:T(8,128)}), f32[17,2048]{1,0:T(8,128)}) %all-reduce.2.cloned.1.call-update) | async-done | bytes 139280 | tf_op jit(solution)/shard_map/psum | solution.py:142
  579.9 1.4 slice.69
  581.4 1.6 slice_bitcast_fusion
  583.0 22.2 %all-gather.18.cloned.1.call-done = bf16[256,2048]{1,0:T(8,128)(2,1)} async-done(((bf16[32,2048]{1,0:T(8,128)(2,1)}), bf16[256,2048]{1,0:T(8,128)(2,1)}) %all-gather.18.cloned.1.call-update) | async-done | bytes 1048592 | tf_op jit(solution)/shard_map/all_gather | solution.py:148
  605.2 2.3 copy.78
  607.5 4.4 all-to-all-start.1
  611.8 2.0 convolution_convert_fusion.2
  614.6 1.6 fusion.39
  616.2 2.0 fusion.38
  618.2 10.8 %all-to-all-done.1 = bf16[256,4,512]{2,0,1:T(8,128)(2,1)} async-done(((bf16[256,4,512]{2,0,1:T(8,128)(2,1)}), bf16[256,4,512]{2,0,1:T(8,128)(2,1)}, u32[]{:S(2)}, u32[]{:S(2)}) %all-to-all-start.1) | async-done | bytes 1048608 | tf_op jit(solution)/shard_map/all_to_all | solution.py:149
  629.0 4.2 all-to-all-start.2
  633.3 2.5 fusion.37
  635.8 2.2 fusion.36
  639.8 11.8 %all-gather.20.cloned.1.call-done = bf16[1024,512]{0,1:T(8,128)(2,1)} async-done(((bf16[256,512]{0,1:T(8,128)(2,1)}), bf16[1024,512]{0,1:T(8,128)(2,1)}) %all-gather.20.cloned.1.call-update) | async-done | bytes 1048592 | tf_op jit(solution)/shard_map/all_gather | solution.py:66
  651.6 3.2 fusion.117
  654.8 68.7 %all-gather.22.cloned.1.call-done = bf16[2,1024,1536]{2,1,0:T(8,128)(2,1)} async-done(((bf16[2,256,1536]{2,1,0:T(8,128)(2,1)}), bf16[2,1024,1536]{2,1,0:T(8,128)(2,1)}) %all-gather.22.cloned.1.call-update) | async-done | bytes 6291472 | tf_op jit(solution)/shard_map/all_gather | solution.py:102
  723.5 9.1 %convolution_bitcast_fusion = f32[2,512,1536]{1,2,0:T(8,128)} fusion(bf16[2,1024,1536]{2,1,0:T(8,128)(2,1)} %all-gather.22.cloned.1.call-done, bf16[1024,512,1]{1,0,2:T(8,128)(2,1)} %bitcast.18), kind=kOutput, calls=%fused_computation.2 | convolution fusion | flops 3221225472 | bytes 13631488 | tf_op jit(solution)/shard_map/td,etf->edf/dot_general | solution.py:129
  732.6 6.6 copy.65
  (147 shorter events, 20.7 us)
Async XLA Ops:
  7.2 18.6 %copy-start = (bf16[512,2048]{1,0:T(8,128)(2,1)S(1)}, bf16[512,2048]{1,0:T(8,128)(2,1)}, u32[]{:S(2)}) copy-start(bf16[512,2048]{1,0:T(8,128)(2,1)} %param.13) | copy-start | bytes 6291460
  7.2 15.2 %copy-start.42 = (bf16[256,512]{1,0:T(8,128)(2,1)S(1)}, bf16[256,512]{1,0:T(8,128)(2,1)}, u32[]{:S(2)}) copy-start(bf16[256,512]{1,0:T(8,128)(2,1)} %param.11) | copy-start | bytes 786436
  7.2 53.3 %reduce-scatter.4.cloned.1.call-start = ((), (), s32[]{:S(2)}) async-start(), calls=%async_computation.7 | async-start | bytes 1179648 | tf_op jit(solution)/shard_map/reduce_scatter | solution.py:67
  19.9 5.5 copy-start.16
  21.1 2.6 copy-start.9
  21.1 2.6 copy-start.31
  23.2 2.2 copy-start.5
  23.2 2.2 copy-start.29
  25.0 2.6 copy-start.12
  25.4 35.1 %copy-start.2 = (bf16[32,2048]{1,0:T(8,128)(2,1)S(1)}, bf16[32,2048]{1,0:T(8,128)(2,1)}, u32[]{:S(2)}) copy-start(bf16[32,2048]{1,0:T(8,128)(2,1)} %param.10) | copy-start | bytes 393220
  25.4 36.8 %copy-start.21 = (f32[2048]{0:T(1024)S(1)}, f32[2048]{0:T(1024)}, u32[]{:S(2)}) copy-start(f32[2048]{0:T(1024)} %param.14) | copy-start | bytes 24580
  25.8 38.7 %copy-start.14 = (bf16[256,128]{0,1:T(8,128)(2,1)}, bf16[256,128]{0,1:T(8,128)(2,1)S(1)}, u32[]{:S(2)}) copy-start(bf16[256,128]{0,1:T(8,128)(2,1)S(1)} %fusion.35) | copy-start | bytes 196612
  27.5 37.6 %copy-start.24 = (s32[32,8]{0,1:T(8,128)S(1)}, s32[32,8]{0,1:T(8,128)}, u32[]{:S(2)}) copy-start(s32[32,8]{0,1:T(8,128)} %param.18) | copy-start | bytes 3076
  27.5 55.0 %all-gather.16.cloned.1.call-start = ((), (), s32[]{:S(2)}) async-start(), calls=%async_computation.12 | async-start | bytes 1179648 | tf_op jit(solution)/shard_map/all_gather | solution.py:38
  28.3 78.4 %all-gather.10.cloned.1.call-start = ((), (), s32[]{:S(2)}) async-start(), calls=%async_computation.8 | async-start | bytes 1179648 | tf_op jit(solution)/shard_map/all_gather | solution.py:78
  62.2 17.3 %copy-start.22 = (f32[32]{0:T(128)}, f32[32]{0:T(128)S(1)}, u32[]{:S(2)}) copy-start(f32[32]{0:T(128)S(1)} %get-tuple-element.57) | copy-start | bytes 388
  63.9 166.5 %all-gather.12.cloned.1.call-start = ((), (), s32[]{:S(2)}) async-start(), calls=%async_computation.9 | async-start | bytes 15728640 | tf_op jit(solution)/shard_map/all_gather | solution.py:39
  64.5 42.2 %copy-start.19 = (bf16[2048,16]{0,1:T(8,128)(2,1)S(1)}, bf16[2048,16]{0,1:T(8,128)(2,1)}, u32[]{:S(2)}) copy-start(bf16[2048,16]{0,1:T(8,128)(2,1)} %param.15) | copy-start | bytes 196612
  64.5 237.6 %all-gather.14.cloned.1.call-start = ((), (), s32[]{:S(2)}) async-start(), calls=%async_computation.10 | async-start | bytes 7864320 | tf_op jit(solution)/shard_map/all_gather | solution.py:40
  65.1 289.1 %reduce-scatter.8.cloned.1.call-start = ((), (), s32[]{:S(2)}) async-start(), calls=%async_computation.13 | async-start | bytes 1179648 | tf_op jit(solution)/shard_map/reduce_scatter | solution.py:106
  108.3 231.9 %copy-start.20 = (f32[256,16]{0,1:T(8,128)}, f32[256,16]{0,1:T(8,128)S(1)}, u32[]{:S(2)}) copy-start(f32[256,16]{0,1:T(8,128)S(1)} %fusion.107) | copy-start | bytes 49156
  321.4 66.6 %reduce-scatter.6.cloned.1.call-start = ((), (), s32[]{:S(2)}) async-start(), calls=%async_computation.11 | async-start | bytes 1179648 | tf_op jit(solution)/shard_map/reduce_scatter | solution.py:116
  321.5 18.8 %copy-start.4 = (bf16[32,2048]{1,0:T(8,128)(2,1)S(1)}, bf16[32,2048]{1,0:T(8,128)(2,1)}, u32[]{:S(2)}) copy-start(bf16[32,2048]{1,0:T(8,128)(2,1)} %multiply_convert_fusion.6) | copy-start | bytes 393220
  321.5 32.7 %copy-start.3 = (bf16[32,2048]{1,0:T(8,128)(2,1)S(1)}, bf16[32,2048]{1,0:T(8,128)(2,1)}, u32[]{:S(2)}) copy-start(bf16[32,2048]{1,0:T(8,128)(2,1)} %reduce-scatter.4.cloned.1.call-done) | copy-start | bytes 393220
  328.5 120.6 %all-gather.24.cloned.1.call-start = ((), (), s32[]{:S(2)}) async-start(), calls=%async_computation.17 | async-start | bytes 5242880 | tf_op jit(solution)/shard_map/all_gather | solution.py:41
  329.9 10.2 %all-to-all-start = ((f32[2,8,32]{2,0,1:T(2,128)}), f32[2,8,32]{2,0,1:T(2,128)S(1)}, u32[]{:S(2)}, u32[]{:S(2)}) async-start(f32[2,8,32]{2,0,1:T(2,128)} %copy.52), calls=%async_computation.3 | async-start | bytes 16384 | tf_op jit(solution)/shard_map/all_to_all | solution.py:115
  334.5 245.4 %all-reduce.2.cloned.1.call-start = ((), (), s32[]{:S(2)}) async-start(), calls=%async_computation.18 | async-start | bytes 393216 | tf_op jit(solution)/shard_map/psum | solution.py:142
  357.9 247.3 %all-gather.18.cloned.1.call-start = ((), (), s32[]{:S(2)}) async-start(), calls=%async_computation.14 | async-start | bytes 1179648 | tf_op jit(solution)/shard_map/all_gather | solution.py:148
  388.0 6.0 copy-start.32
  388.0 6.0 copy-start.40
  389.9 261.7 %all-gather.20.cloned.1.call-start = ((), (), s32[]{:S(2)}) async-start(), calls=%async_computation.15 | async-start | bytes 1310720 | tf_op jit(solution)/shard_map/all_gather | solution.py:66
  391.5 332.0 %all-gather.22.cloned.1.call-start = ((), (), s32[]{:S(2)}) async-start(), calls=%async_computation.16 | async-start | bytes 7864320 | tf_op jit(solution)/shard_map/all_gather | solution.py:102
  394.0 8.2 %copy-start.26 = (f32[256]{0:T(256)S(1)}, f32[256]{0:T(256)}, u32[]{:S(2)}) copy-start(f32[256]{0:T(256)} %copy-done.25) | copy-start | bytes 3076
  394.0 8.2 %copy-start.34 = (f32[256]{0:T(256)S(1)}, f32[256]{0:T(256)}, u32[]{:S(2)}) copy-start(f32[256]{0:T(256)} %copy-done.33) | copy-start | bytes 3076
  394.0 8.8 %copy-start.28 = (f32[256]{0:T(256)S(1)}, f32[256]{0:T(256)}, u32[]{:S(2)}) copy-start(f32[256]{0:T(256)} %copy-done.27) | copy-start | bytes 3076
  394.0 8.8 %copy-start.36 = (f32[256]{0:T(256)S(1)}, f32[256]{0:T(256)}, u32[]{:S(2)}) copy-start(f32[256]{0:T(256)} %copy-done.35) | copy-start | bytes 3076
  394.0 9.3 %copy-start.30 = (f32[256]{0:T(256)S(1)}, f32[256]{0:T(256)}, u32[]{:S(2)}) copy-start(f32[256]{0:T(256)} %copy-done.29) | copy-start | bytes 3076
  394.0 9.3 %copy-start.38 = (f32[256]{0:T(256)S(1)}, f32[256]{0:T(256)}, u32[]{:S(2)}) copy-start(f32[256]{0:T(256)} %copy-done.37) | copy-start | bytes 3076
  394.0 9.9 %copy-start.1 = (bf16[256,2048]{1,0:T(8,128)(2,1)S(1)}, bf16[256,2048]{1,0:T(8,128)(2,1)}, u32[]{:S(2)}) copy-start(bf16[256,2048]{1,0:T(8,128)(2,1)} %all-gather.10.cloned.1.call-done) | copy-start | bytes 3145732
  397.7 20.7 %all-to-all-start.3 = ((bf16[2,768,256]{2,0,1:T(2,128)(2,1)}), bf16[2,768,256]{2,0,1:T(2,128)(2,1)}, u32[]{:S(2)}, u32[]{:S(2)}) async-start(bf16[2,768,256]{2,0,1:T(2,128)(2,1)} %copy.61), calls=%async_computation.6 | async-start | bytes 1572864 | tf_op jit(solution)/shard_map/all_to_all | solution.py:123
  607.5 6.4 copy-start.13
  607.5 6.4 copy-start.15
  607.5 7.1 copy-start.10
  607.5 21.6 %all-to-all-start.1 = ((bf16[256,4,512]{2,0,1:T(8,128)(2,1)}), bf16[256,4,512]{2,0,1:T(8,128)(2,1)}, u32[]{:S(2)}, u32[]{:S(2)}) async-start(bf16[256,4,512]{2,0,1:T(8,128)(2,1)} %bitcast.83), calls=%async_computation.4 | async-start | bytes 2097152 | tf_op jit(solution)/shard_map/all_to_all | solution.py:149
  614.6 18.7 %copy-start.18 = (bf16[256,512]{0,1:T(8,128)(2,1)S(1)}, bf16[256,512]{0,1:T(8,128)(2,1)}, u32[]{:S(2)}) copy-start(bf16[256,512]{0,1:T(8,128)(2,1)} %copy-done.17) | copy-start | bytes 786436
  616.2 19.6 %copy-start.6 = (f32[256,1024]{0,1:T(8,128)S(1)}, f32[256,1024]{0,1:T(8,128)}, u32[]{:S(2)}) copy-start(f32[256,1024]{0,1:T(8,128)} %copy-done.5) | copy-start | bytes 3145732
  616.2 19.6 %copy-start.41 = (f32[256]{0:T(256)S(1)}, f32[256]{0:T(256)}, u32[]{:S(2)}) copy-start(f32[256]{0:T(256)} %log_add_fusion) | copy-start | bytes 3076
  629.0 25.8 %all-to-all-start.2 = ((bf16[256,4,512]{2,0,1:T(8,128)(2,1)}), bf16[256,4,512]{2,0,1:T(8,128)(2,1)}, u32[]{:S(2)}, u32[]{:S(2)}) async-start(bf16[256,4,512]{2,0,1:T(8,128)(2,1)} %bitcast.82), calls=%async_computation.5 | async-start | bytes 2097152 | tf_op jit(solution)/shard_map/all_to_all | solution.py:79
  (11 other events, 13.7 us)
Sparse Core Ops, SparseCore 0:
  27.6 32.8 reduce-scatter.3
  62.1 20.3 all-gather.15
  84.7 21.9 all-gather.9
  108.3 121.9 all-gather.11
  232.0 70.0 all-gather.13
  321.6 32.5 reduce-scatter.7
  357.0 30.9 reduce-scatter.5
  389.9 59.2 all-gather.23
  455.3 124.6 all-reduce.1
  582.0 23.1 all-gather.17
  607.0 44.5 all-gather.19
  653.9 69.5 all-gather.21
where the time goes:
time: 747 us; the launch traced here: 746 us
  waiting for transfers between devices  573 us (77%)
  matrix products  74 us (10%)
  blocking collectives  25.9 us (3%)
  local copies, waits for them, and re-layouts  21.9 us (3%)
  other arithmetic  18.3 us (2%)
  starting transfers between devices  18.1 us (2%)
  between operations  14.8 us (2%)
    psum x1, waiting for transfers between devices, per_device(): lax.psum(jnp.concatenate([router_term, gain_term], axis=0), ('ctx', 'exp'))  125 us
    all_gather x1, waiting for transfers between devices, per_device(): gate_up_full = lax.all_gather(expert_gate_up, 'ctx', axis=1, tiled=True)  122 us
    all_gather x1, waiting for transfers between devices, per_device(): pair_grad_all = lax.all_gather(pair_grad, 'ctx', axis=1, tiled=True)  68.7 us
    all_gather x1, waiting for transfers between devices, per_device(): down_full = lax.all_gather(expert_down, 'ctx', axis=1, tiled=True)  61.8 us
    reduce_scatter x1, waiting for transfers between devices, per_device(): lax.psum_scatter(jnp.dot(attention_flat, out_weight, preferred_element_ty...  32.2 us
    reduce_scatter x1, waiting for transfers between devices, per_device(): lax.psum_scatter(jnp.sum(probs_cols * expert_out, axis=0).astype(jnp.bflo...  30.1 us
    all_gather x1, waiting for transfers between devices, per_device(): upstream_all = lax.all_gather(upstream_block, 'ctx', axis=0, tiled=True)  29.4 us
    all_gather x1, waiting for transfers between devices, per_device(): arriving = lax.all_gather(input_grad, 'exp', axis=0, tiled=True)  22.2 us
  transfers between devices with their start and end apart: 16, of which 15 were waited for; matrix products, arithmetic and copies ran while one was open for 9% of the time, Pallas kernels for 0%

commit v1 on v0

--- a/solution.py
+++ b/solution.py
@@ -139,7 +139,9 @@
         "te,de->td", logit_grad, router_weight.astype(jnp.float32), precision=lax.Precision.HIGHEST
     )
     gain_term = jnp.sum(normed_grad * residual * inv_rms, axis=0, keepdims=True)
-    summed = lax.psum(jnp.concatenate([router_term, gain_term], axis=0), ("ctx", "exp"))
+    own = jnp.concatenate([router_term, gain_term], axis=0)
+    shards = lax.all_gather(own, ("ctx", "exp"), axis=0, tiled=False)
+    summed = shards.sum(axis=0)
     router_grad, gain_grad = (summed[:EXPERTS].T, summed[EXPERTS])
     inner_mean = jnp.mean(residual * norm_gain * normed_grad, axis=1, keepdims=True)
     input_grad = (

time: 747 us -> 673 us (0.901)
  waiting for transfers between devices: 573 us -> 499 us
    psum x1 -> x0, waiting for transfers between devices: 125 us -> none  [per_device(): lax.psum(jnp.concatenate([router_term, gain_term], axis=0), ('ctx', 'exp'))]
    all_gather x0 -> x1, waiting for transfers between devices: none -> 56.5 us  [per_device(): shards = lax.all_gather(own, ('ctx', 'exp'), axis=0, tiled=False)]
  transfers between devices with their start and end apart: 16 -> 16, of which waited for: 15 -> 15; matrix products, arithmetic and copies ran while one was open for 9% -> 12% of each run, Pallas kernels for 0% -> 0%
where the time goes in v1:
time: 673 us; the launch traced here: 672 us
  waiting for transfers between devices  499 us (74%)
  matrix products  74.1 us (11%)
  blocking collectives  25.8 us (4%)
  local copies, waits for them, and re-layouts  20.3 us (3%)
  other arithmetic  19.5 us (3%)
  starting transfers between devices  18.1 us (3%)
  between operations  14.8 us (2%)
    all_gather x1, waiting for transfers between devices, per_device(): gate_up_full = lax.all_gather(expert_gate_up, 'ctx', axis=1, tiled=True)  122 us
    all_gather x1, waiting for transfers between devices, per_device(): pair_grad_all = lax.all_gather(pair_grad, 'ctx', axis=1, tiled=True)  69.9 us
    all_gather x1, waiting for transfers between devices, per_device(): down_full = lax.all_gather(expert_down, 'ctx', axis=1, tiled=True)  61.8 us
    all_gather x1, waiting for transfers between devices, per_device(): shards = lax.all_gather(own, ('ctx', 'exp'), axis=0, tiled=False)  56.5 us
    reduce_scatter x1, waiting for transfers between devices, per_device(): lax.psum_scatter(jnp.sum(probs_cols * expert_out, axis=0).astype(jnp.bflo...  32.4 us
    reduce_scatter x1, waiting for transfers between devices, per_device(): lax.psum_scatter(jnp.dot(attention_flat, out_weight, preferred_element_ty...  32.2 us
    all_gather x1, waiting for transfers between devices, per_device(): upstream_all = lax.all_gather(upstream_block, 'ctx', axis=0, tiled=True)  29.4 us
    all_gather x1, waiting for transfers between devices, per_device(): normed_block = lax.all_gather(normed, 'exp', axis=0, tiled=True)  21.3 us
  transfers between devices with their start and end apart: 16, of which 15 were waited for; matrix products, arithmetic and copies ran while one was open for 12% of the time, Pallas kernels for 0%

profile of v1, /device:TPU:0, one launch (start us, length us, event | category | flops | bytes accessed | tf_op | source)
XLA Modules:
  0.0 671.7 jit_solution(9229757774867903891)
XLA Ops:
  8.3 11.5 %all_gather.36 = bf16[1024,256]{1,0:T(8,128)(2,1)S(1)} all-gather(bf16[256,256]{1,0:T(8,128)(2,1)S(1)} %constant_dynamic-slice_fusion), channel_id=1, replica_groups=mesh['ctx'=4,'exp'=8] {'ctx'}, dimensions={0}, use_global_device_ids=true | all-gather | bytes 655360 | tf_op jit(solution)/shard_map/all_gather | solution.py:36
  19.9 1.3 fusion.115
  21.1 1.3 fusion.114
  25.6 1.7 convolution_convert_fusion.1
  28.1 32.2 %reduce-scatter.4.cloned.1.call-done = bf16[32,2048]{1,0:T(8,128)(2,1)} async-done(((bf16[256,2048]{1,0:T(8,128)(2,1)}), bf16[32,2048]{1,0:T(8,128)(2,1)}) %reduce-scatter.4.cloned.1.call-update) | async-done | bytes 131088 | tf_op jit(solution)/shard_map/reduce_scatter | solution.py:67
  61.4 1.7 multiply_convert_fusion.6
  64.4 14.3 %all-gather.1 = s32[8,32,8]{1,2,0:T(8,128)S(1)} all-gather(s32[1,32,8]{1,2,0:T(8,128)S(1)} %bitcast.95), channel_id=1, replica_groups=mesh['ctx'=4,'exp'=8] {'exp'}, dimensions={0}, use_global_device_ids=true | all-gather | bytes 9216 | tf_op jit(solution)/shard_map/all_gather | solution.py:37
  78.7 3.8 all-gather.19.cloned.1.call-done
  82.5 2.8 convert_element_type.151
  85.3 21.3 %all-gather.13.cloned.1.call-done = bf16[256,2048]{1,0:T(8,128)(2,1)} async-done(((bf16[32,2048]{1,0:T(8,128)(2,1)}), bf16[256,2048]{1,0:T(8,128)(2,1)}) %all-gather.13.cloned.1.call-update) | async-done | bytes 1048592 | tf_op jit(solution)/shard_map/all_gather | solution.py:78
  106.6 1.6 fusion.116
  108.3 122.0 %all-gather.15.cloned.1.call-done = bf16[2,2048,1536]{2,1,0:T(8,128)(2,1)} async-done(((bf16[2,512,1536]{2,1,0:T(8,128)(2,1)}), bf16[2,2048,1536]{2,1,0:T(8,128)(2,1)}) %all-gather.15.cloned.1.call-update) | async-done | bytes 12582928 | tf_op jit(solution)/shard_map/all_gather | solution.py:39
  230.4 10.0 %convolution_bitcast_fusion.1 = f32[2,256,1536]{2,1,0:T(8,128)} fusion(bf16[2,2048,1536]{2,1,0:T(8,128)(2,1)} %all-gather.15.cloned.1.call-done, bf16[256,2048]{1,0:T(8,128)(2,1)} %all-gather.13.cloned.1.call-done), kind=kOutput, calls=%fused_computation.8 | convolution fusion | flops 3221225472 | bytes 16777216 | tf_op jit(solution)/shard_map/td,edf->etf/dot_general | solution.py:90
  240.3 61.8 %all-gather.17.cloned.1.call-done = bf16[2,768,2048]{2,1,0:T(8,128)(2,1)} async-done(((bf16[2,192,2048]{2,1,0:T(8,128)(2,1)}), bf16[2,768,2048]{2,1,0:T(8,128)(2,1)}) %all-gather.17.cloned.1.call-update) | async-done | bytes 6291472 | tf_op jit(solution)/shard_map/all_gather | solution.py:40
  302.1 9.4 %multiply_convert_fusion.4 = (bf16[2,256,768]{2,1,0:T(8,128)(2,1)S(1)}, bf16[2,256,768]{2,1,0:T(8,128)(2,1)S(1)}, bf16[2,768,256]{1,2,0:T(8,128)(2,1)}, bf16[2,256,768]{2,1,0:T(8,128)(2,1)}) fusion(f32[2,256,1536]{2,1,0:T(8,128)} %convolution_bitcast_fusion.1, f32[2,256]{1,0:T(2,128)S(1)} %dynamic-slice_bitcast_fusion, ...), kind=kOutput, calls=%fused_computation.20 | convolution fusion | flops 1620180992 | bytes 14684160 | tf_op jit(solution)/shard_map/etd,efd->etf/dot_general | solution.py:98
  312.7 9.0 %fusion.4 = bf16[256,2048]{1,0:T(8,128)(2,1)} fusion(bf16[2,2048,1536]{2,1,0:T(8,128)(2,1)} %all-gather.15.cloned.1.call-done, bf16[2,256,768]{2,1,0:T(8,128)(2,1)S(1)} %get-tuple-element.51, bf16[2,256,768]{2,1,0:T(8,128)(2,1)S(1)} %get-tuple-element.50), kind=kOutput, calls=%fused_computation.12 | convolution fusion | flops 3224895488 | bytes 15204352 | tf_op jit(solution)/shard_map/etf,edf->td/dot_general | solution.py:103
  321.8 7.0 %fusion.1 = (f32[2,256]{1,0:T(2,128)S(1)}, bf16[256,2048]{1,0:T(8,128)(2,1)}) fusion(f32[256,2048]{1,0:T(8,128)} %convert_element_type.151, f32[2,256]{1,0:T(2,128)S(1)} %dynamic-slice_bitcast_fusion, bf16[2,256,768]{2,1,0:T(8,128)(2,1)} %get-tuple-element.53, bf16[2,768,2048]{2,1,0:T(8,128)(2,1)} %all-gather.17.cloned.1.call-done), kind=kOutput, calls=%fused_computation.4 | convolution fusion | flops 1616379392 | bytes 10227712 | tf_op jit(solution)/shard_map/etf,efd->etd/dot_general | solution.py:110
  330.2 4.6 all-to-all-start
  334.9 5.6 all-to-all-done
  340.5 13.9 %reduce-scatter.8.cloned.1.call-done = bf16[32,2048]{1,0:T(8,128)(2,1)} async-done(((bf16[256,2048]{1,0:T(8,128)(2,1)}), bf16[32,2048]{1,0:T(8,128)(2,1)}) %reduce-scatter.8.cloned.1.call-update) | async-done | bytes 131088 | tf_op jit(solution)/shard_map/reduce_scatter | solution.py:106
  354.5 1.5 multiply_reduce_fusion
  356.0 32.4 %reduce-scatter.6.cloned.1.call-done = bf16[32,2048]{1,0:T(8,128)(2,1)} async-done(((bf16[256,2048]{1,0:T(8,128)(2,1)}), bf16[32,2048]{1,0:T(8,128)(2,1)}) %reduce-scatter.6.cloned.1.call-update) | async-done | bytes 131088 | tf_op jit(solution)/shard_map/reduce_scatter | solution.py:116
  388.4 1.8 subtract_convert_fusion
  391.0 2.6 pad_maximum_fusion
  395.6 1.2 log_add_fusion.3
  396.8 3.0 copy.61
  399.8 4.4 all-to-all-start.3
  407.1 11.6 %all-to-all-done.3 = bf16[2,768,256]{2,0,1:T(2,128)(2,1)} async-done(((bf16[2,768,256]{2,0,1:T(2,128)(2,1)}), bf16[2,768,256]{2,0,1:T(2,128)(2,1)}, u32[]{:S(2)}, u32[]{:S(2)}) %all-to-all-start.3) | async-done | bytes 786464 | tf_op jit(solution)/shard_map/all_to_all | solution.py:123
  418.7 1.2 copy.62
  420.0 29.4 %all-gather.27.cloned.1.call-done = bf16[1024,2048]{1,0:T(8,128)(2,1)} async-done(((bf16[256,2048]{1,0:T(8,128)(2,1)}), bf16[1024,2048]{1,0:T(8,128)(2,1)}) %all-gather.27.cloned.1.call-update) | async-done | bytes 4194320 | tf_op jit(solution)/shard_map/all_gather | solution.py:41
  449.5 5.6 fusion.2
  455.1 18.8 %all-gather.21.cloned.1.call-done = bf16[256,2048]{1,0:T(8,128)(2,1)} async-done(((bf16[32,2048]{1,0:T(8,128)(2,1)}), bf16[256,2048]{1,0:T(8,128)(2,1)}) %all-gather.21.cloned.1.call-update) | async-done | bytes 1048592 | tf_op jit(solution)/shard_map/all_gather | solution.py:150
  473.9 2.3 copy.78
  476.2 4.4 all-to-all-start.1
  480.6 2.0 convolution_convert_fusion.2
  483.3 1.6 fusion.39
  485.0 2.0 fusion.38
  487.0 10.8 %all-to-all-done.1 = bf16[256,4,512]{2,0,1:T(8,128)(2,1)} async-done(((bf16[256,4,512]{2,0,1:T(8,128)(2,1)}), bf16[256,4,512]{2,0,1:T(8,128)(2,1)}, u32[]{:S(2)}, u32[]{:S(2)}) %all-to-all-start.1) | async-done | bytes 1048608 | tf_op jit(solution)/shard_map/all_to_all | solution.py:151
  497.8 4.3 all-to-all-start.2
  502.0 2.5 fusion.37
  504.6 2.2 fusion.36
  508.5 6.5 all-gather.23.cloned.1.call-done
  515.1 3.2 fusion.117
  518.3 69.9 %all-gather.25.cloned.1.call-done = bf16[2,1024,1536]{2,1,0:T(8,128)(2,1)} async-done(((bf16[2,256,1536]{2,1,0:T(8,128)(2,1)}), bf16[2,1024,1536]{2,1,0:T(8,128)(2,1)}) %all-gather.25.cloned.1.call-update) | async-done | bytes 6291472 | tf_op jit(solution)/shard_map/all_gather | solution.py:102
  588.2 9.1 %convolution_bitcast_fusion = f32[2,512,1536]{1,2,0:T(8,128)} fusion(bf16[2,1024,1536]{2,1,0:T(8,128)(2,1)} %all-gather.25.cloned.1.call-done, bf16[1024,512,1]{1,0,2:T(8,128)(2,1)} %bitcast.18), kind=kOutput, calls=%fused_computation.2 | convolution fusion | flops 3221225472 | bytes 13631488 | tf_op jit(solution)/shard_map/td,etf->edf/dot_general | solution.py:129
  597.3 6.6 copy.65
  603.9 56.5 %all-gather.29.cloned.1.call-done = f32[32,17,2048]{2,1,0:T(8,128)} async-done(((f32[1,17,2048]{2,1,0:T(8,128)}), f32[32,17,2048]{2,1,0:T(8,128)}) %all-gather.29.cloned.1.call-update) | async-done | bytes 4456464 | tf_op jit(solution)/shard_map/all_gather | solution.py:143
  660.4 3.2 reduce_sum.159
  (138 shorter events, 19.4 us)
Async XLA Ops:
  7.2 18.4 %copy-start = (bf16[512,2048]{1,0:T(8,128)(2,1)S(1)}, bf16[512,2048]{1,0:T(8,128)(2,1)}, u32[]{:S(2)}) copy-start(bf16[512,2048]{1,0:T(8,128)(2,1)} %param.13) | copy-start | bytes 6291460
  7.2 15.2 %copy-start.37 = (bf16[256,512]{1,0:T(8,128)(2,1)S(1)}, bf16[256,512]{1,0:T(8,128)(2,1)}, u32[]{:S(2)}) copy-start(bf16[256,512]{1,0:T(8,128)(2,1)} %param.11) | copy-start | bytes 786436
  7.2 53.2 %reduce-scatter.4.cloned.1.call-start = ((), (), s32[]{:S(2)}) async-start(), calls=%async_computation.7 | async-start | bytes 1179648 | tf_op jit(solution)/shard_map/reduce_scatter | solution.py:67
  19.9 5.3 copy-start.13
  21.1 2.6 copy-start.9
  21.1 2.6 copy-start.28
  22.4 1.6 copy-start.8
  22.8 1.8 copy-start.7
  22.8 1.8 copy-start.24
  23.2 2.0 copy-start.5
  23.2 2.0 copy-start.26
  24.6 2.7 copy-start.31
  25.2 36.2 %copy-start.33 = (f32[256]{0:T(256)}, f32[256]{0:T(256)S(1)}, u32[]{:S(2)}) copy-start(f32[256]{0:T(256)S(1)} %fusion.55) | copy-start | bytes 3076
  25.2 35.1 %copy-start.2 = (bf16[32,2048]{1,0:T(8,128)(2,1)S(1)}, bf16[32,2048]{1,0:T(8,128)(2,1)}, u32[]{:S(2)}) copy-start(bf16[32,2048]{1,0:T(8,128)(2,1)} %param.10) | copy-start | bytes 393220
  25.2 36.2 %copy-start.19 = (f32[2048]{0:T(1024)S(1)}, f32[2048]{0:T(1024)}, u32[]{:S(2)}) copy-start(f32[2048]{0:T(1024)} %param.14) | copy-start | bytes 24580
  27.3 37.1 %copy-start.21 = (s32[32,8]{0,1:T(8,128)S(1)}, s32[32,8]{0,1:T(8,128)}, u32[]{:S(2)}) copy-start(s32[32,8]{0,1:T(8,128)} %param.18) | copy-start | bytes 3076
  27.3 55.2 %all-gather.19.cloned.1.call-start = ((), (), s32[]{:S(2)}) async-start(), calls=%async_computation.12 | async-start | bytes 1179648 | tf_op jit(solution)/shard_map/all_gather | solution.py:38
  28.1 78.6 %all-gather.13.cloned.1.call-start = ((), (), s32[]{:S(2)}) async-start(), calls=%async_computation.8 | async-start | bytes 1179648 | tf_op jit(solution)/shard_map/all_gather | solution.py:78
  63.1 167.2 %all-gather.15.cloned.1.call-start = ((), (), s32[]{:S(2)}) async-start(), calls=%async_computation.9 | async-start | bytes 15728640 | tf_op jit(solution)/shard_map/all_gather | solution.py:39
  63.7 42.9 %copy-start.17 = (bf16[2048,16]{0,1:T(8,128)(2,1)S(1)}, bf16[2048,16]{0,1:T(8,128)(2,1)}, u32[]{:S(2)}) copy-start(bf16[2048,16]{0,1:T(8,128)(2,1)} %param.15) | copy-start | bytes 196612
  63.7 238.4 %all-gather.17.cloned.1.call-start = ((), (), s32[]{:S(2)}) async-start(), calls=%async_computation.10 | async-start | bytes 7864320 | tf_op jit(solution)/shard_map/all_gather | solution.py:40
  64.3 290.2 %reduce-scatter.8.cloned.1.call-start = ((), (), s32[]{:S(2)}) async-start(), calls=%async_computation.13 | async-start | bytes 1179648 | tf_op jit(solution)/shard_map/reduce_scatter | solution.py:106
  108.3 246.2 %copy-start.18 = (f32[256,16]{0,1:T(8,128)}, f32[256,16]{0,1:T(8,128)S(1)}, u32[]{:S(2)}) copy-start(f32[256,16]{0,1:T(8,128)S(1)} %fusion.107) | copy-start | bytes 49156
  321.7 66.6 %reduce-scatter.6.cloned.1.call-start = ((), (), s32[]{:S(2)}) async-start(), calls=%async_computation.11 | async-start | bytes 1179648 | tf_op jit(solution)/shard_map/reduce_scatter | solution.py:116
  321.8 32.7 %copy-start.3 = (bf16[32,2048]{1,0:T(8,128)(2,1)S(1)}, bf16[32,2048]{1,0:T(8,128)(2,1)}, u32[]{:S(2)}) copy-start(bf16[32,2048]{1,0:T(8,128)(2,1)} %reduce-scatter.4.cloned.1.call-done) | copy-start | bytes 393220
  321.8 66.6 %copy-start.14 = (bf16[32,2048]{1,0:T(8,128)(2,1)S(1)}, bf16[32,2048]{1,0:T(8,128)(2,1)}, u32[]{:S(2)}) copy-start(bf16[32,2048]{1,0:T(8,128)(2,1)} %param.19) | copy-start | bytes 393220
  328.8 120.7 %all-gather.27.cloned.1.call-start = ((), (), s32[]{:S(2)}) async-start(), calls=%async_computation.17 | async-start | bytes 5242880 | tf_op jit(solution)/shard_map/all_gather | solution.py:41
  330.2 10.2 %all-to-all-start = ((f32[2,8,32]{2,0,1:T(2,128)}), f32[2,8,32]{2,0,1:T(2,128)S(1)}, u32[]{:S(2)}, u32[]{:S(2)}) async-start(f32[2,8,32]{2,0,1:T(2,128)} %copy.52), calls=%async_computation.3 | async-start | bytes 16384 | tf_op jit(solution)/shard_map/all_to_all | solution.py:115
  334.8 139.1 %all-gather.21.cloned.1.call-start = ((), (), s32[]{:S(2)}) async-start(), calls=%async_computation.14 | async-start | bytes 1179648 | tf_op jit(solution)/shard_map/all_gather | solution.py:150
  340.5 50.5 %copy-start.20 = (f32[32]{0:T(128)}, f32[32]{0:T(128)S(1)}, u32[]{:S(2)}) copy-start(f32[32]{0:T(128)S(1)} %multiply_reduce_fusion.7) | copy-start | bytes 388
  388.4 5.4 copy-start.4
  390.1 124.9 %all-gather.23.cloned.1.call-start = ((), (), s32[]{:S(2)}) async-start(), calls=%async_computation.15 | async-start | bytes 1310720 | tf_op jit(solution)/shard_map/all_gather | solution.py:66
  391.0 197.2 %all-gather.25.cloned.1.call-start = ((), (), s32[]{:S(2)}) async-start(), calls=%async_computation.16 | async-start | bytes 7864320 | tf_op jit(solution)/shard_map/all_gather | solution.py:102
  393.6 12.3 %copy-start.1 = (bf16[256,2048]{1,0:T(8,128)(2,1)S(1)}, bf16[256,2048]{1,0:T(8,128)(2,1)}, u32[]{:S(2)}) copy-start(bf16[256,2048]{1,0:T(8,128)(2,1)} %all-gather.13.cloned.1.call-done) | copy-start | bytes 3145732
  393.7 266.7 %all-gather.29.cloned.1.call-start = ((), (), s32[]{:S(2)}) async-start(), calls=%async_computation.18 | async-start | bytes 6488064 | tf_op jit(solution)/shard_map/all_gather | solution.py:143
  394.8 9.5 %copy-start.23 = (f32[256]{0:T(256)S(1)}, f32[256]{0:T(256)}, u32[]{:S(2)}) copy-start(f32[256]{0:T(256)} %copy-done.22) | copy-start | bytes 3076
  394.8 9.5 %copy-start.30 = (f32[256]{0:T(256)S(1)}, f32[256]{0:T(256)}, u32[]{:S(2)}) copy-start(f32[256]{0:T(256)} %copy-done.29) | copy-start | bytes 3076
  394.8 10.0 %copy-start.25 = (f32[256]{0:T(256)S(1)}, f32[256]{0:T(256)}, u32[]{:S(2)}) copy-start(f32[256]{0:T(256)} %copy-done.24) | copy-start | bytes 3076
  394.8 10.0 %copy-start.32 = (f32[256]{0:T(256)S(1)}, f32[256]{0:T(256)}, u32[]{:S(2)}) copy-start(f32[256]{0:T(256)} %copy-done.31) | copy-start | bytes 3076
  394.8 10.6 %copy-start.27 = (f32[256]{0:T(256)S(1)}, f32[256]{0:T(256)}, u32[]{:S(2)}) copy-start(f32[256]{0:T(256)} %copy-done.26) | copy-start | bytes 3076
  394.8 10.6 %copy-start.34 = (f32[256]{0:T(256)S(1)}, f32[256]{0:T(256)}, u32[]{:S(2)}) copy-start(f32[256]{0:T(256)} %copy-done.33) | copy-start | bytes 3076
  399.8 18.9 %all-to-all-start.3 = ((bf16[2,768,256]{2,0,1:T(2,128)(2,1)}), bf16[2,768,256]{2,0,1:T(2,128)(2,1)}, u32[]{:S(2)}, u32[]{:S(2)}) async-start(bf16[2,768,256]{2,0,1:T(2,128)(2,1)} %copy.61), calls=%async_computation.6 | async-start | bytes 1572864 | tf_op jit(solution)/shard_map/all_to_all | solution.py:123
  476.2 7.1 %copy-start.10 = (f32[256,1024]{0,1:T(8,128)S(1)}, f32[256,1024]{0,1:T(8,128)}, u32[]{:S(2)}) copy-start(f32[256,1024]{0,1:T(8,128)} %copy-done.9) | copy-start | bytes 3145732
  476.2 21.6 %all-to-all-start.1 = ((bf16[256,4,512]{2,0,1:T(8,128)(2,1)}), bf16[256,4,512]{2,0,1:T(8,128)(2,1)}, u32[]{:S(2)}, u32[]{:S(2)}) async-start(bf16[256,4,512]{2,0,1:T(8,128)(2,1)} %bitcast.85), calls=%async_computation.4 | async-start | bytes 2097152 | tf_op jit(solution)/shard_map/all_to_all | solution.py:151
  483.3 18.7 %copy-start.16 = (bf16[256,512]{0,1:T(8,128)(2,1)S(1)}, bf16[256,512]{0,1:T(8,128)(2,1)}, u32[]{:S(2)}) copy-start(bf16[256,512]{0,1:T(8,128)(2,1)} %copy-done.15) | copy-start | bytes 786436
  485.0 19.6 %copy-start.6 = (f32[256,1024]{0,1:T(8,128)S(1)}, f32[256,1024]{0,1:T(8,128)}, u32[]{:S(2)}) copy-start(f32[256,1024]{0,1:T(8,128)} %copy-done.5) | copy-start | bytes 3145732
  485.0 19.6 %copy-start.36 = (f32[256]{0:T(256)S(1)}, f32[256]{0:T(256)}, u32[]{:S(2)}) copy-start(f32[256]{0:T(256)} %log_add_fusion) | copy-start | bytes 3076
  497.8 20.5 %all-to-all-start.2 = ((bf16[256,4,512]{2,0,1:T(8,128)(2,1)}), bf16[256,4,512]{2,0,1:T(8,128)(2,1)}, u32[]{:S(2)}, u32[]{:S(2)}) async-start(bf16[256,4,512]{2,0,1:T(8,128)(2,1)} %bitcast.84), calls=%async_computation.5 | async-start | bytes 2097152 | tf_op jit(solution)/shard_map/all_to_all | solution.py:79
  (6 other events, 7.4 us)
Sparse Core Ops, SparseCore 0:
  27.4 32.8 reduce-scatter.3
  62.0 20.5 all-gather.18
  84.7 21.8 all-gather.12
  108.3 121.9 all-gather.14
  232.0 70.0 all-gather.16
  321.8 32.5 reduce-scatter.7
  357.3 30.9 reduce-scatter.5
  390.2 59.2 all-gather.26
  451.6 22.2 all-gather.20
  475.6 39.4 all-gather.22
  517.5 70.6 all-gather.24
  591.1 69.2 all-gather.28
